TPU v7x, 32 devices: a whole 2x2x4 slice. The times are simulated.
32 devices in a mesh: fsdp: 8 (over z, core), seq: 4 (over y, x).
Axes of the slice: x: 2, y: 2, z: 4, core: 2. Of those that a mesh axis runs over, the one named last changes fastest.
Arguments:
- hidden_in: bfloat16 [8192, 1536], P(('fsdp', 'seq')), may hold values from -12 to 12
- cotangent: bfloat16 [8192, 1536], P(('fsdp', 'seq')), may hold values from -6 to 6
- segment_ids: int32 [8, 1024], P('fsdp', 'seq'), may hold values from 0 to 3, never falling along the last dimension, each value on 1 to 512 neighbouring positions
- w_qkv: bfloat16 [1536, 3072], P('fsdp', 'seq'), may hold values from -1.5 to 1.5
- w_out: bfloat16 [1536, 1536], P('fsdp', 'seq'), may hold values from -0.625 to 0.625
- w_gate: bfloat16 [1536, 4096], P('fsdp', 'seq'), may hold values from -0.15625 to 0.15625
- w_up: bfloat16 [1536, 4096], P('fsdp', 'seq'), may hold values from -0.15625 to 0.15625
- w_down: bfloat16 [4096, 1536], P('fsdp', 'seq'), may hold values from -0.09375 to 0.09375
- gain_attn: bfloat16 [1536], P(('fsdp', 'seq')), may hold values from 0.099609375 to 1.8984375
- gain_mlp: bfloat16 [1536], P(('fsdp', 'seq')), may hold values from 0.099609375 to 1.8984375
Outputs:
- output: float32 [8192, 1536], P(('fsdp', 'seq'))
- d_input: float32 [8192, 1536], P(('fsdp', 'seq'))
- g_qkv: float32 [1536, 3072], P('fsdp', 'seq')
- g_out: float32 [1536, 1536], P('fsdp', 'seq')
- g_gate: float32 [1536, 4096], P('fsdp', 'seq')
- g_up: float32 [1536, 4096], P('fsdp', 'seq')
- g_down: float32 [4096, 1536], P('fsdp', 'seq')
- g_gain_attn: float32 [1536], P(('fsdp', 'seq'))
- g_gain_mlp: float32 [1536], P(('fsdp', 'seq'))
Inputs may be any that keep to these rules, and one draw needn't show every extreme that they name: `segment_ids`: document numbers never fall along a row; a document has 1 to 512 tokens.
All inputs are finite; a program needn't handle non-finite values.
Results may differ from a plain program's by a relative error of at most 0.02.
Values may be sent and summed in bfloat16 or wider, within the bound.
A program may use at most 320 MiB of HBM per device.

v0:
```python
import functools
import math

import jax
import jax.numpy as jnp
from jax import lax
from jax.experimental import pallas as pl
from jax.experimental.pallas import tpu as pltpu
from jax.sharding import PartitionSpec as P

HEAD_DIM = 96
EPSILON = 1e-05
ROPE_BASE = 100000.0
NEGATIVE = -1e30
SCALE = 1.0 / math.sqrt(HEAD_DIM)
SCALE_TWO = SCALE * math.log2(math.e)
MESH = pl.DeviceIdType.MESH
BLOCK = 256
F32 = jnp.float32
BF16 = jnp.bfloat16
ANY = pl.BlockSpec(memory_space=pl.ANY)
VMEM = pl.BlockSpec(memory_space=pltpu.VMEM)


def dot(left, right):
    return jnp.dot(left, right, preferred_element_type=F32)


def dot_nt(left, right):
    return lax.dot_general(left, right, (((1,), (1,)), ((), ())), preferred_element_type=F32)


def dot_tn(left, right):
    return lax.dot_general(left, right, (((0,), (0,)), ((), ())), preferred_element_type=F32)


def shape(dims, kind):
    return jax.ShapeDtypeStruct(dims, kind)


def params(collective=None):
    return pltpu.CompilerParams(
        collective_id=collective,
        has_side_effects=collective is not None,
        vmem_limit_bytes=60 << 20,
    )


def cost(flops, moved):
    return pl.CostEstimate(flops=flops, bytes_accessed=moved, transcendentals=0)


def others(size):
    me = lax.axis_index("seq")
    if size == 4:
        low, high = lax.rem(me, 2), me // 2
        return [high * 2 + 1 - low, (1 - high) * 2 + low, (1 - high) * 2 + 1 - low]
    return [lax.rem(me + step, size) for step in range(1, size)]


def meet(seq, fsdp, pairs=(), ends=True):
    barrier = pltpu.get_barrier_semaphore()
    row = lax.axis_index("fsdp")
    for peer in others(seq):
        pl.semaphore_signal(barrier, inc=1, device_id={"seq": peer}, device_id_type=MESH)
    for step in range(1, fsdp):
        peer = lax.rem(row + step, fsdp)
        pl.semaphore_signal(barrier, inc=1, device_id={"fsdp": peer}, device_id_type=MESH)
    for there in pairs:

        @pl.when(away(there))
        def _(there=there):
            pl.semaphore_signal(
                barrier,
                inc=1,
                device_id={"fsdp": there[0], "seq": there[1]},
                device_id_type=MESH,
            )

    if pairs:

        @pl.when(away(pairs[0]))
        def _():
            pl.semaphore_wait(barrier, seq + fsdp - 2 + len(pairs))

        @pl.when(jnp.logical_not(away(pairs[0])))
        def _():
            pl.semaphore_wait(barrier, seq + fsdp - 2)
    elif ends:
        pl.semaphore_wait(barrier, seq + fsdp - 2)


def away(there):
    return jnp.logical_or(
        there[0] != lax.axis_index("fsdp"), there[1] != lax.axis_index("seq")
    )


def flip(one, two):
    return one + two - 2 * one * two


def turn(chip, core, high):
    return flip(chip // 2, core) * 2 + flip(lax.rem(chip, 2), flip(high, core))


def row_owner(seq, fsdp):
    row, me = lax.axis_index("fsdp"), lax.axis_index("seq")
    if seq == 4 and fsdp == 8:
        chip, core = row // 2, lax.rem(row, 2)
        to = (turn(chip, core, me // 2) * 2 + lax.rem(me, 2), chip)
        first = flip(me // 2, chip // 2)
        high = flip(flip(lax.rem(me, 2), lax.rem(chip, 2)), first)
        return to, (me * 2 + first, high * 2 + core)
    ratio = fsdp // seq
    to = (lax.rem(row, ratio) * seq + me, row // ratio)
    source = (me * ratio + row // seq, lax.rem(row, seq))
    return to, source


def line_place(seq, fsdp, down, across):
    if seq == 4 and fsdp == 8:
        return turn(lax.axis_index("seq"), down, across // 2) * 2 + across % 2
    return down * seq + across


def push(src, dst, sems, index, peer, axis="seq", slot=None):
    return pltpu.make_async_remote_copy(
        src_ref=src,
        dst_ref=dst,
        send_sem=sems[0].at[index],
        recv_sem=sems[1].at[index if slot is None else slot],
        device_id={axis: peer},
        device_id_type=MESH,
    )


class Move:
    def __init__(self, src, dst, to, sems, bounce):
        self.src, self.dst, self.to, self.sems, self.bounce = src, dst, to, sems, bounce
        self.index = 0

    def remote(self):
        return pltpu.make_async_remote_copy(
            src_ref=self.src,
            dst_ref=self.dst,
            send_sem=self.sems[0].at[self.index],
            recv_sem=self.sems[1].at[self.index],
            device_id={"fsdp": self.to[0], "seq": self.to[1]},
            device_id_type=MESH,
        )

    def within(self, last):
        src, dst = (self.bounce, self.dst) if last else (self.src, self.bounce)
        return pltpu.make_async_copy(src, dst, self.sems[2].at[0])

    def start(self):
        @pl.when(away(self.to))
        def _():
            self.remote().start()

        @pl.when(jnp.logical_not(away(self.to)))
        def _():
            self.within(False).start()

    def finish(self):
        @pl.when(away(self.to))
        def _():
            self.remote().wait()

        @pl.when(jnp.logical_not(away(self.to)))
        def _():
            self.within(False).wait()
            self.within(True).start()
            self.within(True).wait()


class Home:
    def __init__(self, seq, fsdp, own, mid, out, sems):
        self.seq, self.fsdp = seq, fsdp
        self.own, self.mid, self.out, self.sems = own, mid, out, sems
        me, row = lax.axis_index("seq"), lax.axis_index("fsdp")
        self.me, self.row = me, row
        owner = row_owner(seq, fsdp)[1]
        self.stop = owner[1]
        if seq == 4 and fsdp == 8:
            chip, core = row // 2, lax.rem(row, 2)
            self.slot = lax.rem(owner[0], 2)
            self.takes = lax.rem(me, 2) == core
            self.items = [(turn(chip, k, me // 2), turn(chip, k, me // 2) * 2 + k) for k in (0, 1)]
            self.origin = turn(chip, core, me // 2) * 2 + lax.rem(me, 2)
        else:
            ratio = fsdp // seq
            self.slot = me
            self.takes = me == lax.rem(row, seq)
            self.items = [(k, k * ratio + row // seq) for k in range(seq)]
            self.origin = lax.rem(row, ratio) * seq + me

    def plane(self):
        return push(self.own, self.mid.at[self.slot], self.sems, 0, self.stop, "seq", self.slot)

    def plane_local(self):
        return pltpu.make_async_copy(self.own, self.mid.at[self.slot], self.sems[2].at[0])

    def start_plane(self):
        @pl.when(self.me != self.stop)
        def _():
            self.plane().start()

        @pl.when(self.me == self.stop)
        def _():
            self.plane_local().start()

    def finish_plane(self):
        @pl.when(self.me != self.stop)
        def _():
            self.plane().wait_send()

        @pl.when(self.me == self.stop)
        def _():
            self.plane_local().wait()

        @pl.when(self.takes)
        def _():
            for k, (column, _) in enumerate(self.items):

                @pl.when(column != self.me)
                def _(k=k, column=column):
                    push(self.own, self.mid.at[k], self.sems, 0, column, "seq", k).wait_recv()

    def line(self, k, row):
        return push(self.mid.at[k], self.out, self.sems, k, row, "fsdp", len(self.items))

    def each_line(self, remote, local):
        @pl.when(self.takes)
        def _():
            for k, (_, row) in enumerate(self.items):

                @pl.when(row != self.row)
                def _(k=k, row=row):
                    remote(self.line(k, row))

                @pl.when(row == self.row)
                def _(k=k):
                    local(pltpu.make_async_copy(self.mid.at[k], self.out, self.sems[2].at[0]))

    def start_line(self):
        self.each_line(lambda copy: copy.start(), lambda copy: copy.start())

    def finish_line(self):
        @pl.when(self.origin != self.row)
        def _():
            self.line(0, self.origin).wait_recv()

        self.each_line(lambda copy: copy.wait_send(), lambda copy: copy.wait())


def home_count(seq, fsdp):
    return 2 if seq == 4 and fsdp == 8 else seq


def home_sems(seq, fsdp):
    dma = pltpu.SemaphoreType.DMA
    count = home_count(seq, fsdp)
    return [dma((count,)), dma((count + 1,)), dma((1,))]


def chips(row):
    chip, core = row // 2, lax.rem(row, 2)
    pair = chip // 2
    mate = pair * 2 + 1 - lax.rem(chip, 2)
    first = (1 - pair) * 2
    return chip, core, mate, first, first + 1


def inner_chip(chip):
    return jnp.logical_or(chip == 1, chip == 2)


def line_scratch(fsdp):
    dma = pltpu.SemaphoreType.DMA
    return [dma((max(fsdp, 9),)), dma((max(fsdp, 8),)), dma((1,))]


class LineGather:
    def __init__(self, fsdp, own, whole, sems, part=None, bounce=None):
        self.fsdp, self.own, self.whole, self.sems = fsdp, own, whole, sems
        self.bounce = bounce
        if part is not None:
            self.own, self.whole = own.at[part], whole.at[:, part]
        self.row = lax.axis_index("fsdp")
        if fsdp == 8:
            self.chip, self.core, self.mate, self.one, self.two = chips(self.row)
            self.near = 2 - self.chip // 2

    def at(self, chip):
        return chip * 2 + self.core

    def send(self, slot, index, peer, own=False):
        src = self.own if own else self.whole.at[slot]
        return push(src, self.whole.at[slot], self.sems, index, peer, "fsdp", slot)

    def arrive(self, slot):
        self.send(slot, 0, self.row).wait_recv()

    def local(self):
        src = self.own if self.bounce is None else self.bounce
        return pltpu.make_async_copy(src, self.whole.at[self.row], self.sems[2].at[0])

    def start_local(self):
        if self.bounce is None:
            self.local().start()
        else:
            pltpu.make_async_copy(self.own, self.bounce, self.sems[2].at[0]).start()

    def settle(self):
        if self.bounce is not None:
            pltpu.make_async_copy(self.own, self.bounce, self.sems[2].at[0]).wait()
            self.local().start()

    def sibling(self, chip, index):
        return self.send(self.at(chip), index, self.chip * 2 + 1 - self.core)

    def start(self):
        if self.fsdp != 8:
            for step in range(1, self.fsdp):
                peer = lax.rem(self.row + step, self.fsdp)
                self.send(self.row, step - 1, peer, own=True).start()
        else:
            self.send(self.row, 1, self.at(self.near), own=True).start()
            self.send(self.row, 0, self.at(self.mate), own=True).start()
            self.send(self.row, 2, self.chip * 2 + 1 - self.core, own=True).start()
        self.start_local()

    def pass_on(self, index, chip):
        self.arrive(self.at(chip))

        @pl.when(inner_chip(self.chip))
        def _():
            self.send(self.at(chip), index, self.at(self.mate)).start()

        self.sibling(chip, index + 3).start()

    def forward(self):
        self.settle()
        if self.fsdp == 8:

            @pl.when(inner_chip(self.chip))
            def _():
                self.pass_on(3, self.one)
                self.pass_on(4, self.two)

    def finish(self):
        if self.fsdp != 8:
            for step in range(1, self.fsdp):
                self.arrive(lax.rem(self.row - step + self.fsdp, self.fsdp))
            for step in range(1, self.fsdp):
                self.send(self.row, step - 1, self.row, own=True).wait_send()
            self.local().wait()
            return
        self.arrive(self.at(self.mate))
        self.sibling(self.mate, 5).start()

        @pl.when(jnp.logical_not(inner_chip(self.chip)))
        def _():
            self.pass_on(3, self.one)
            self.pass_on(4, self.two)

        for chip in range(4):
            self.arrive(chip * 2 + 1 - self.core)
        self.local().wait()
        for index in range(3):
            self.send(self.row, index, self.row, own=True).wait_send()
        for index, chip in ((5, self.mate), (6, self.one), (7, self.two)):
            self.sibling(chip, index).wait_send()

        @pl.when(inner_chip(self.chip))
        def _():
            self.send(self.at(self.one), 3, self.row).wait_send()
            self.send(self.at(self.two), 4, self.row).wait_send()


def mine_scratch(fsdp, height, width):
    count = 4 if fsdp == 8 else 1
    return [pltpu.VMEM((count, height, width), BF16), pltpu.SemaphoreType.DMA((count,))]


def reduce_scratch(fsdp, height, width):
    if fsdp == 8:
        bufs = [pltpu.VMEM((4, height, width), BF16)] * 2
    else:
        bufs = [pltpu.VMEM((1, 16, 128), BF16), pltpu.VMEM((fsdp - 1, height, width), BF16)]
    return bufs + line_scratch(fsdp)


class LineReduce:
    def __init__(self, fsdp, grad, pair, got, *sems, mine=None):
        self.fsdp, self.grad, self.pair, self.got, self.sems = fsdp, grad, pair, got, sems
        self.row = lax.axis_index("fsdp")
        if fsdp == 8:
            self.chip, self.core, self.mate, self.one, self.two = chips(self.row)
            self.roles = [self.one, self.two, self.mate, self.chip]
            self.own = [role * 2 + self.core for role in self.roles]
        else:
            self.own = [self.row]
        self.mine = mine

    def fetch(self, role):
        return pltpu.make_async_copy(
            self.grad.at[self.own[role]], self.mine[0].at[role], self.mine[1].at[role]
        )

    def block(self, role, part):
        if self.mine is not None:
            return self.mine[0][role, part].astype(F32)
        return self.grad[self.own[role], part].astype(F32)

    def ready(self, role):
        if self.mine is not None:
            self.fetch(role).wait()

    def rows(self, task):
        height = self.grad.shape[1]
        step = 64
        while height % step:
            step //= 2
        each(height, step, lambda at: task(pl.ds(at, step)))

    def across(self, role):
        other = 1 - self.core
        return push(
            self.grad.at[self.roles[role] * 2 + other],
            self.pair.at[role],
            self.sems,
            role,
            self.chip * 2 + other,
            "fsdp",
        )

    def to_mate(self, role):
        slot = (1, 2, 0)[role]
        return push(
            self.pair.at[role],
            self.got.at[slot],
            self.sems,
            4 + slot,
            self.mate * 2 + self.core,
            "fsdp",
        )

    def to_other(self, role):
        return push(
            self.pair.at[role],
            self.got.at[3],
            self.sems,
            7 + role,
            self.roles[role] * 2 + self.core,
            "fsdp",
            7,
        )

    def direct(self, step):
        peer = lax.rem(self.row + step, self.fsdp)
        return push(
            self.grad.at[peer], self.got.at[step - 1], self.sems, step - 1, peer, "fsdp"
        )

    def start(self):
        if self.fsdp != 8:
            for step in range(1, self.fsdp):
                self.direct(step).start()
        else:
            for role in range(4):
                self.across(role).start()
        if self.mine is not None:
            for role in range(len(self.own)):
                self.fetch(role).start()

    def pairs(self):
        if self.fsdp != 8:
            return
        for role in range(3):
            self.across(role).wait_recv()
            self.ready(role)

            def add(part, role=role):
                self.pair[role, part] = (
                    self.pair[role, part].astype(F32) + self.block(role, part)
                ).astype(BF16)

            self.rows(add)
            if role < 2:

                @pl.when(jnp.logical_not(inner_chip(self.chip)))
                def _(role=role):
                    self.to_mate(role).start()
            else:
                self.to_mate(role).start()

    def forward(self, roles=(0, 1)):
        if self.fsdp != 8:
            return

        @pl.when(inner_chip(self.chip))
        def _():
            for role in roles:
                self.to_mate(role).wait_recv()

                def add(part, role=role):
                    self.pair[role, part] = (
                        self.pair[role, part].astype(F32) + self.got[role + 1, part].astype(F32)
                    ).astype(BF16)

                self.rows(add)
                self.to_other(role).start()

    def finish(self, out, offset=0):
        height = self.grad.shape[1]
        if offset or out.shape[0] != height:
            out = out.at[pl.ds(offset, height)]
        if self.fsdp != 8:
            for step in range(1, self.fsdp):
                self.direct(step).wait_recv()

            self.ready(0)

            def total(part):
                value = self.block(0, part)
                for step in range(1, self.fsdp):
                    value = value + self.got[step - 1, part].astype(F32)
                out[part, :] = value.astype(out.dtype)

            self.rows(total)
            for step in range(1, self.fsdp):
                self.direct(step).wait_send()
            return
        self.across(3).wait_recv()
        self.to_mate(2).wait_recv()
        self.to_other(0).wait_recv()
        self.ready(3)

        def total(part):
            out[part, :] = (
                self.block(3, part)
                + self.pair[3, part].astype(F32)
                + self.got[0, part].astype(F32)
                + self.got[3, part].astype(F32)
            ).astype(out.dtype)

        self.rows(total)
        for role in range(4):
            self.across(role).wait_send()
        self.to_mate(2).wait_send()

        @pl.when(inner_chip(self.chip))
        def _():
            self.to_other(0).wait_send()
            self.to_other(1).wait_send()

        @pl.when(jnp.logical_not(inner_chip(self.chip)))
        def _():
            self.to_mate(0).wait_send()
            self.to_mate(1).wait_send()


def n_copies(size):
    return 6 if size == 4 else size - 1


class Gather:
    def __init__(self, size, own, whole, sems):
        self.size, self.own, self.whole, self.sems = size, own, whole, sems
        self.me = lax.axis_index("seq")
        self.peers = others(size)
        self.rows = own.shape[0]

    def place(self, device, half=None):
        count = self.rows // 2 if half is not None else self.rows
        at = device * self.rows + (count if half else 0)
        return self.whole.at[pl.ds(pl.multiple_of(at, count), count)]

    def copy(self, index):
        me, own, sems = self.me, self.own, self.sems
        if self.size != 4:
            return push(own, self.place(me), sems, index, self.peers[index])
        side, over, _ = self.peers
        count = self.rows // 2
        one, two = pl.ds(0, count), pl.ds(count, count)
        src, dst, peer = [
            (own.at[one], self.place(me, 0), side),
            (own.at[two], self.place(me, 1), side),
            (own.at[two], self.place(me, 1), over),
            (own.at[one], self.place(me, 0), over),
            (self.place(side, 0), self.place(side, 0), over),
            (self.place(over, 1), self.place(over, 1), side),
        ][index]
        return push(src, dst, sems, index, peer)

    def local(self, sem):
        return pltpu.make_async_copy(self.own, self.place(self.me), sem)

    def start(self):
        for index in (0, 2, 1, 3) if self.size == 4 else range(self.size - 1):
            self.copy(index).start()

    def forward(self):
        if self.size == 4:
            for index in (0, 2):
                self.copy(index).wait_recv()
            self.copy(4).start()
            self.copy(5).start()

    def order(self):
        if self.size == 4:
            return [(self.peers[0], (1,)), (self.peers[1], (3,)), (self.peers[2], (4, 5))]
        return [
            (lax.rem(self.me - k - 1 + self.size, self.size), (k,)) for k in range(self.size - 1)
        ]

    def coming(self, index):
        if self.size == 4:
            return flip(self.me // 2, index // 2) * 2 + flip(
                lax.rem(self.me, 2), lax.rem(index, 2)
            )
        return lax.rem(self.me - index + self.size, self.size)

    def arrive(self, number):
        for index in self.order()[number - 1][1]:
            self.copy(index).wait_recv()

    def sent(self):
        for index in range(n_copies(self.size)):
            self.copy(index).wait_send()

    def finish(self, task=None):
        for number, (device, _) in enumerate(self.order()):
            self.arrive(number + 1)
            if task is not None:
                task(device)
        self.sent()


def scatter_scratch(size, rows, width):
    small = size == 4
    return [
        pltpu.VMEM((size, rows, width), BF16),
        pltpu.VMEM((2, rows // 2, width) if small else (1, 16, 128), BF16),
        pltpu.VMEM((2 if small else size - 1, rows, width), BF16),
    ] + [pltpu.SemaphoreType.DMA((n_copies(size),))] * 2


class Scatter:
    def __init__(self, size, held, stage, got, sems):
        self.size, self.held, self.stage, self.got, self.sems = size, held, stage, got, sems
        self.me = lax.axis_index("seq")
        self.peers = others(size)
        half = held.shape[1] // 2
        self.parts = [pl.ds(0, half), pl.ds(half, half)]

    def copy(self, index):
        held, stage, got, sems = self.held, self.stage, self.got, self.sems
        if self.size != 4:
            peer = self.peers[index]
            return push(held.at[peer], got.at[index], sems, index, peer)
        side, over, far = self.peers
        one, two = self.parts
        src, dst, peer = [
            (held.at[far, one], stage.at[0], side),
            (held.at[far, two], stage.at[1], over),
            (held.at[side, one], got.at[0, one], side),
            (held.at[over, two], got.at[1, two], over),
            (held.at[side, two], got.at[0, two], side),
            (held.at[over, one], got.at[1, one], over),
        ][index]
        return push(src, dst, sems, index, peer)

    def sends(self):
        if self.size == 4:
            return [(2, (0, 1)), (0, (2,)), (1, (3,))]
        return [(k, (k,)) for k in range(self.size - 1)]

    def units(self):
        rows = self.held.shape[1]
        return (8, rows // 2) if self.size == 4 else (self.size, rows)

    def unit(self, index):
        if self.size != 4:
            return lax.rem(self.me + index + 1, self.size), 0
        half, k = index // 4, lax.rem(index, 4)
        one, two = 1 - k // 2, 1 - lax.rem(k, 2)
        low, high = one + half * (two - one), two + half * (one - two)
        return flip(self.me // 2, high) * 2 + flip(lax.rem(self.me, 2), low), half

    def unit_made(self, index):
        starts = {0: 0, 1: 2, 4: 1, 5: 3}
        if self.size != 4:
            starts = {k: k for k in range(self.size - 1)}
        for number, copy in starts.items():

            @pl.when(index == number)
            def _(copy=copy):
                self.copy(copy).start()

    def send(self, make, hooks=()):
        hooks = list(hooks)
        for place, indices in self.sends():
            make(self.peers[place], self.held.at[self.peers[place]])
            for index in indices:
                self.copy(index).start()
            run_hook(hooks)
        while hooks:
            run_hook(hooks)

    def forward_one(self, stage, device, half, index):
        if self.size == 4:
            self.copy(stage).wait_recv()
            spot = (device, self.parts[half])
            total = self.held[spot].astype(F32) + self.stage[stage].astype(F32)
            self.held[spot] = total.astype(BF16)
            self.copy(index).start()

    def forward_side(self):
        self.forward_one(1, self.peers[0], 1, 4)

    def forward_over(self):
        self.forward_one(0, self.peers[1], 0, 5)

    def forward(self):
        self.forward_side()
        self.forward_over()

    def finish(self):
        for index in range(n_copies(self.size)):
            if self.size != 4 or index > 1:
                self.copy(index).wait_recv()
        for index in range(n_copies(self.size)):
            self.copy(index).wait_send()

    def terms(self, rows):
        total = self.got[0, rows].astype(F32)
        for k in range(1, self.got.shape[0]):
            total = total + self.got[k, rows].astype(F32)
        return total


def run_hook(hooks):
    if hooks:
        hook = hooks.pop(0)
        if hook is not None:
            hook()


def at_step(index, tasks):
    for number, task in tasks.items():

        @pl.when(index == number)
        def _(task=task):
            task()


def each(count, step, task):
    def run(index, carry):
        task(pl.multiple_of(index * step, step))
        return carry

    lax.fori_loop(0, count // step, run, 0)


class Load:
    def __init__(self, src, dst, sem):
        self.dst, self.waited = dst, False
        self.copy = pltpu.make_async_copy(src, dst, sem)
        self.copy.start()

    def get(self):
        if not self.waited:
            self.waited = True
            self.copy.wait()
        return self.dst


def loads(srcs, dsts, sems):
    return [Load(src, dst, sems.at[k]) for k, (src, dst) in enumerate(zip(srcs, dsts))]


def load_scratch(arrays):
    return [pltpu.VMEM(array.shape, array.dtype) for array in arrays] + [
        pltpu.SemaphoreType.DMA((len(arrays),))
    ]


def tile_of(width, most):
    tile = most
    while width % tile:
        tile //= 2
    return tile


def swap_halves(block):
    half = HEAD_DIM // 2
    return jnp.concatenate([block[:, half:], block[:, :half]], axis=1)


def inv_rms(values):
    return lax.rsqrt(jnp.mean(values * values, axis=-1, keepdims=True) + EPSILON)


def mask_bias(ids_col, ids_row, start, low, rows, span):
    query = start + lax.broadcasted_iota(jnp.int32, (rows, span), 0)
    key = low + lax.broadcasted_iota(jnp.int32, (rows, span), 1)
    same = ids_col[pl.ds(start, rows), :] == ids_row[:, pl.ds(low, span)]
    bias = jnp.where(jnp.logical_and(same, key <= query), 0.0, NEGATIVE)
    return jnp.concatenate([bias, bias], axis=0)


def join_blocks(blocks, seq, whole):
    fsdp = blocks.shape[0]
    ratio = fsdp // seq
    height, width = blocks.shape[1:]
    for down in range(ratio):
        for across in range(seq):
            whole[down * height : (down + 1) * height, across * width : (across + 1) * width] = (
                blocks[line_place(seq, fsdp, down, across)]
            )


def forward_kernel(
    seq, fsdp, hidden, w_qkv, w_out, w_gate, w_up, w_down, cot, ids, gain_one, gain_two, ids_row,
    ids_col, gains, attn, lse, middle, own_normed, normed_out, cosine_out, sine_out, packed_out,
    rows_out_out, cols_qkv_out, cols_gate, cols_up, moved_out, moved_down, cot_all, raw, ids_all,
    gain_own, gain_parts, blocks_out, held, stage, got, normed, cosine, sine, packed, rows_out,
    cols_qkv, own_cot, own_gate, own_up, own_out, own_down, *sems
):
    def take(count):
        nonlocal sems
        taken, sems = sems[:count], sems[count:]
        return taken

    rows, width = hidden.shape
    length = rows * seq
    groups = w_qkv.shape[1] // (4 * HEAD_DIM)
    me, row = lax.axis_index("seq"), lax.axis_index("fsdp")
    to, source = row_owner(seq, fsdp)
    share = gain_one.shape[1]
    tile = tile_of(width, 512)
    gain_own[0:1, :] = gain_one[...].astype(F32)
    gain_own[1:2, :] = gain_two[...].astype(F32)
    gain_parts[row, me] = gain_own[...]
    ids_all[me] = ids[...]
    meet(seq, fsdp, (to, source))
    local, out_sems = take(2)
    stores = []

    def store(src, dst):
        stores.append(pltpu.make_async_copy(src, dst, out_sems.at[len(stores)]))
        stores[-1].start()

    whole = Gather(seq, hidden, raw, take(2))
    cots = Gather(seq, cot, cot_all, take(2))
    sums = Scatter(seq, held, stage, got, take(2))
    half = w_gate.shape[0] // 2
    one, two = pl.ds(0, half), pl.ds(half, half)
    line_qkv = LineGather(fsdp, w_qkv, cols_qkv, take(3))
    line_out = LineGather(fsdp, moved_out, blocks_out, take(3))
    line_gate = [
        LineGather(fsdp, w_gate, cols_gate, take(3), part, own_gate.at[part])
        for part in (one, two)
    ]
    line_up = [
        LineGather(fsdp, w_up, cols_up, take(3), part, own_up.at[part]) for part in (one, two)
    ]
    move_out = Move(w_out, moved_out, to, take(3), own_out)
    move_down = Move(w_down, moved_down, to, take(3), own_down)
    id_sems, gain_sems, wide_sems = take(2), take(2), take(2)
    id_copies = [
        push(ids, ids_all.at[me], id_sems, k, peer) for k, peer in enumerate(others(seq))
    ]
    gain_copies = [
        push(gain_own, gain_parts.at[row, me], gain_sems, k, peer)
        for k, peer in enumerate(others(seq))
    ]
    for copy in id_copies + gain_copies:
        copy.start()
    line_qkv.start()
    whole.start()
    move_out.start()
    mine = whole.local(local.at[0])
    mine.start()
    cot_in = pltpu.make_async_copy(cot, own_cot, local.at[1])
    cot_in.start()
    for copy in gain_copies:
        copy.wait()
    wide = [
        push(
            gain_parts.at[row],
            gain_parts.at[row],
            wide_sems,
            step - 1,
            lax.rem(row + step, fsdp),
            "fsdp",
        )
        for step in range(1, fsdp)
    ]
    for copy in wide:
        copy.start()
    for copy in id_copies:
        copy.wait()
    for k in range(seq):
        for at in range(0, rows, 128):
            piece = ids_all[k, :, at : at + 128]
            ids_row[:, k * rows + at : k * rows + at + 128] = piece
            turned = jnp.transpose(jnp.broadcast_to(piece, (128, 128)))
            ids_col[k * rows + at : k * rows + at + 128, :] = turned[:, :1]
    whole.forward()
    line_qkv.forward()
    for line in line_gate:
        line.start()
    order = lax.broadcasted_iota(jnp.int32, (1, HEAD_DIM // 2), 1).astype(F32)
    inverse = jnp.exp(order * (-2.0 * math.log(ROPE_BASE) / HEAD_DIM))

    def table(at):
        part = pl.ds(at, BLOCK)
        first = jnp.sum(
            (ids_row[...] < ids_col[part, :]).astype(jnp.int32).astype(F32),
            axis=-1,
            keepdims=True,
        )
        place = (at + lax.broadcasted_iota(jnp.int32, (BLOCK, 1), 0)).astype(F32) - first
        angles = place * inverse
        cos, sin = jnp.cos(angles), jnp.sin(angles)
        cosine[part, :] = jnp.concatenate([cos, cos], axis=1)
        sine[part, :] = jnp.concatenate([-sin, sin], axis=1)

    each(length, BLOCK, table)
    for copy in wide:
        copy.wait()
    for r in range(fsdp):
        for k in range(seq):
            at = (r * seq + k) * share
            gains[:, at : at + share] = gain_parts[r, k]
    mine.wait()

    def norm(device):
        base = pl.multiple_of(device * rows, rows)

        def part(at):
            values = raw[pl.ds(base + at, 128), :].astype(F32)
            normed[pl.ds(base + at, 128), :] = (
                values * inv_rms(values) * gains[0:1, :]
            ).astype(BF16)

        each(rows, 128, part)

    norm(me)
    move_out.finish()
    line_out.start()
    whole.finish(norm)
    cots.start()
    cot_in.wait()
    kept = pltpu.make_async_copy(own_cot, cots.place(me), local.at[0])
    kept.start()
    line_out.forward()
    line_gate[0].forward()
    for line in line_up:
        line.start()
    move_down.start()
    store(normed, normed_out)
    store(cosine, cosine_out)
    store(sine, sine_out)
    line_qkv.finish()
    store(cols_qkv, cols_qkv_out)
    for group in range(groups):

        def project(at, group=group):
            part = pl.ds(at, 512)
            low = group * 4 * HEAD_DIM
            weight = cols_qkv[:, :, low : low + 4 * HEAD_DIM].reshape(width, 4 * HEAD_DIM)
            proj = dot(normed[part, :], weight)
            for slot in range(4):
                piece = proj[:, slot * HEAD_DIM : (slot + 1) * HEAD_DIM]
                if slot < 3:
                    piece = piece * cosine[part, :] + swap_halves(piece) * sine[part, :]
                packed[group * 4 + slot, part, :] = piece.astype(BF16)

        each(length, 512, project)
    store(packed, packed_out)
    line_out.finish()
    join_blocks(blocks_out, seq, rows_out)
    store(rows_out, rows_out_out)
    hooks = {
        0: line_gate[1].forward,
        1: cots.forward,
        3: line_up[0].forward,
        5: sums.forward_over,
        6: line_up[1].forward,
    }
    count, unit_rows = sums.units()
    span = length // 2 + unit_rows

    def unit(index):
        device, half = sums.unit(index)
        start = pl.multiple_of(device * rows + half * unit_rows, unit_rows)
        low = pl.multiple_of(jnp.maximum(start - length // 2, 0), unit_rows)
        part, keys = pl.ds(start, unit_rows), pl.ds(low, span)
        spot = pl.ds(pl.multiple_of(half * unit_rows, unit_rows), unit_rows)
        bias = mask_bias(ids_col, ids_row, start, low, unit_rows, span)
        mixed, logs = [], []
        for group in range(groups):
            queries = jnp.concatenate(
                [packed[group * 4, part, :], packed[group * 4 + 1, part, :]], axis=0
            )
            scores = dot_nt(queries, packed[group * 4 + 2, keys, :]) * SCALE_TWO + bias
            most = jnp.max(scores, axis=-1, keepdims=True)
            grown = jnp.exp2(scores - most)
            total = jnp.sum(grown, axis=-1, keepdims=True)
            weights = (grown * (1.0 / total)).astype(BF16)
            out = dot(weights, packed[group * 4 + 3, keys, :])
            log_total = most + jnp.log2(total)
            mixed += [out[:unit_rows], out[unit_rows:]]
            logs += [log_total[:unit_rows], log_total[unit_rows:]]
        attn[part, :] = jnp.concatenate(mixed, axis=1).astype(BF16)
        lane = lax.broadcasted_iota(jnp.int32, (unit_rows, 128), 1)
        stats = jnp.zeros((unit_rows, 128), F32)
        for head, log_total in enumerate(logs):
            stats = jnp.where(lane == head, log_total, stats)
        lse[part, :] = stats

        def onward(at):
            cols = pl.ds(at, tile)
            term = dot(attn[part, :], rows_out[:, cols])

            @pl.when(device == me)
            def _():
                middle[spot, cols] = raw[part, cols].astype(F32) + term

            @pl.when(device != me)
            def _():
                held[device, spot, cols] = term.astype(BF16)

        each(width, tile, onward)
        sums.unit_made(index)
        for number, hook in hooks.items():

            @pl.when(index == number)
            def _(hook=hook):
                hook()

    each(count, 1, unit)
    sums.forward_side()
    cots.finish()
    kept.wait()
    line_gate[0].finish()
    line_gate[1].finish()
    line_up[0].finish()
    sums.finish()

    def second(at):
        part = pl.ds(at, 128)
        values = middle[part, :] + sums.terms(part)
        middle[part, :] = values
        own_normed[part, :] = (values * inv_rms(values) * gains[1:2, :]).astype(BF16)

    each(rows, 128, second)
    line_up[1].finish()
    move_down.finish()
    for copy in stores:
        copy.wait()


def forward(seq, fsdp, hidden, w_qkv, w_out, w_gate, w_up, w_down, cot, ids, gain_one, gain_two):
    rows, width = hidden.shape
    length = rows * seq
    dma = pltpu.SemaphoreType.DMA
    share = gain_one.shape[1]
    groups = w_qkv.shape[1] // (4 * HEAD_DIM)
    inner = groups * 2 * HEAD_DIM
    return pl.pallas_call(
        functools.partial(forward_kernel, seq, fsdp),
        out_shape=(
            shape((1, length), jnp.int32),
            shape((length, 1), jnp.int32),
            shape((2, width), F32),
            shape((length, inner), BF16),
            shape((length, 128), F32),
            shape((rows, width), F32),
            shape((rows, width), BF16),
            shape((length, width), BF16),
            shape((length, HEAD_DIM), F32),
            shape((length, HEAD_DIM), F32),
            shape((groups * 4, length, HEAD_DIM), BF16),
            shape((inner, width), BF16),
            shape((fsdp,) + w_qkv.shape, BF16),
            shape((fsdp,) + w_gate.shape, BF16),
            shape((fsdp,) + w_up.shape, BF16),
            shape(w_out.shape, BF16),
            shape(w_down.shape, BF16),
            shape((length, width), BF16),
        ),
        in_specs=[ANY] * 7 + [VMEM] * 3,
        out_specs=(VMEM,) * 7 + (ANY,) * 11,
        scratch_shapes=[
            pltpu.VMEM((length, width), BF16),
            pltpu.VMEM((seq, 1, rows), jnp.int32),
            pltpu.VMEM((2, share), F32),
            pltpu.VMEM((fsdp, seq, 2, share), F32),
            pltpu.VMEM((fsdp,) + w_out.shape, BF16),
        ]
        + scatter_scratch(seq, rows, width)[:3]
        + [
            pltpu.VMEM((length, width), BF16),
            pltpu.VMEM((length, HEAD_DIM), F32),
            pltpu.VMEM((length, HEAD_DIM), F32),
            pltpu.VMEM((groups * 4, length, HEAD_DIM), BF16),
            pltpu.VMEM((inner, width), BF16),
            pltpu.VMEM((fsdp,) + w_qkv.shape, BF16),
            pltpu.VMEM(cot.shape, BF16),
            pltpu.VMEM(w_gate.shape, BF16),
            pltpu.VMEM(w_up.shape, BF16),
            pltpu.VMEM(w_out.shape, BF16),
            pltpu.VMEM(w_down.shape, BF16),
        ]
        + [dma((2,)), dma((6,))]
        + [dma((n_copies(seq),))] * 6
        + line_scratch(fsdp) * 6
        + [dma((1,))] * 6
        + [dma((seq - 1,))] * 4
        + [dma((fsdp - 1,))] * 2,
        compiler_params=params(0),
        name="forward",
    )(hidden, w_qkv, w_out, w_gate, w_up, w_down, cot, ids, gain_one, gain_two)


def feed_kernel(
    seq, fsdp, own_normed, cot_all, w_gate, w_up, middle, w_down, gains, d_middle, own_low, d_gain,
    own_down, out_terms, g_gate, g_up, normed, whole_down, blocks, g_down, gate, up, hid, d_gate,
    d_up, held, stage, got, grad_tiles, *rest
):
    arrays, rest = rest[:5], rest[5:]
    rows, width = middle.shape
    length = rows * seq
    inner = gate.shape[1]
    me = lax.axis_index("seq")
    tile = tile_of(width, 512)
    wide = tile_of(inner, 512)
    w_gate, w_up, cot, middle = loads((w_gate, w_up, cot_all, middle), arrays[:4], arrays[4])
    meet(seq, fsdp)
    local, tile_sems = rest[0], rest[1]
    whole = Gather(seq, own_normed, normed, rest[2:4])
    sums = Scatter(seq, held, stage, got, rest[4:6])
    half = w_down.shape[0] // 2
    line_down = [
        LineGather(fsdp, w_down, blocks, rest[6:9], pl.ds(0, half)),
        LineGather(fsdp, w_down, blocks, rest[9:12], pl.ds(half, half)),
    ]
    early = fsdp == 8
    if not early:
        g_down = blocks
    line = LineReduce(fsdp, g_down, *rest[12:])
    for exchange in line_down:
        exchange.start()
    whole.start()
    mine = whole.local(local.at[0])
    mine.start()
    w_gate, w_up = w_gate.get(), w_up.get()
    mine.wait()

    def block_of(device):
        return pl.ds(pl.multiple_of(device * rows, rows), rows)

    def first(device):
        block = block_of(device)

        def part(at):
            cols = pl.ds(at, wide)
            gate_part = dot(normed[block, :], w_gate[:, cols])
            up_part = dot(normed[block, :], w_up[:, cols])
            gate[block, cols] = gate_part
            up[block, cols] = up_part
            hid[block, cols] = (gate_part / (1.0 + jnp.exp(-gate_part)) * up_part).astype(BF16)

        each(inner, wide, part)

    first(me)
    whole.forward()
    hooks = [line_down[0].forward, line_down[1].forward]

    def arrived(device):
        first(device)
        run_hook(hooks)

    whole.finish(arrived)
    while hooks:
        run_hook(hooks)
    cot, middle = cot.get(), middle.get()
    height, across = g_down.shape[1:]

    def down_grad(k):
        cols = slice(k * across, (k + 1) * across)
        for down in range(fsdp // seq):
            g_down[line_place(seq, fsdp, down, k)] = dot_tn(
                hid[:, down * height : (down + 1) * height], cot[:, cols]
            ).astype(BF16)

    def join_down():
        for exchange in line_down:
            exchange.finish()
        join_blocks(blocks, seq, whole_down)

    if not early:
        join_down()
    for k in range(seq):
        down_grad(k)
    line.start()
    if early:
        join_down()

    def second(device, out):
        block = block_of(device)

        def part(at):
            cols = pl.ds(at, wide)
            d_hid = dot_nt(cot[block, :], whole_down[cols, :])
            gate_part = gate[block, cols]
            sig = 1.0 / (1.0 + jnp.exp(-gate_part))
            d_gate[block, cols] = (
                d_hid * up[block, cols] * sig * (1.0 + gate_part * (1.0 - sig))
            ).astype(BF16)
            d_up[block, cols] = (d_hid * (gate_part * sig)).astype(BF16)

        each(inner, wide, part)

        def term(at):
            cols = pl.ds(at, tile)
            total = dot_nt(d_gate[block, :], w_gate[cols, :]) + dot_nt(
                d_up[block, :], w_up[cols, :]
            )
            out[:, cols] = total.astype(out.dtype)

        each(width, tile, term)

    sums.send(second, [None, line.pairs])
    second(me, d_middle)
    sums.forward()
    line.forward((0,))
    wide_rows = grad_tiles.shape[1]
    for left, grads in ((d_gate, g_gate), (d_up, g_up)):

        def tile_out(index, grads=grads):
            return pltpu.make_async_copy(
                grad_tiles.at[lax.rem(index, 2)],
                grads.at[pl.ds(pl.multiple_of(index * wide_rows, wide_rows), wide_rows)],
                tile_sems.at[lax.rem(index, 2)],
            )

        def job(index, left=left, tile_out=tile_out):
            @pl.when(index >= 2)
            def _():
                tile_out(index - 2).wait()

            at = pl.multiple_of(index * wide_rows, wide_rows)
            grad_tiles[lax.rem(index, 2)] = dot_tn(
                normed[:, pl.ds(at, wide_rows)], left[...]
            ).astype(BF16)
            tile_out(index).start()

        count = width // wide_rows
        each(count, 1, job)
        for index in range(max(0, count - 2), count):
            tile_out(index).wait()
        if left is d_gate:
            line.forward((1,))

    def outward(index):
        block = pl.ds(pl.multiple_of(index * rows, rows), rows)

        def part(at):
            cols = pl.ds(at, tile)
            normed[block, cols] = dot(hid[block, :], whole_down[:, cols]).astype(BF16)

        each(width, tile, part)

    each(seq, 1, outward)
    terms_out = pltpu.make_async_copy(normed, out_terms, local.at[0])
    terms_out.start()
    sums.finish()
    d_gain[...] = jnp.zeros_like(d_gain)
    base = pl.multiple_of(me * rows, rows)

    def norm(at):
        part = pl.ds(at, 128)
        values = middle[part, :]
        grad = d_middle[part, :] + sums.terms(part)
        scale = inv_rms(values)
        weighted = grad * gains[1:2, :]
        mean = jnp.mean(weighted * values, axis=-1, keepdims=True)
        d_gain[...] += jnp.sum(grad * values * scale, axis=0, keepdims=True)
        total = cot[pl.ds(base + at, 128), :].astype(F32) + scale * (
            weighted - values * (scale * scale) * mean
        )
        d_middle[part, :] = total
        own_low[part, :] = total.astype(BF16)

    each(rows, 128, norm)
    line.finish(own_down)
    terms_out.wait()


def feed(seq, fsdp, own_normed, cot_all, w_gate, w_up, middle, w_down, gains):
    rows, width = middle.shape
    length = rows * seq
    inner = w_gate.shape[1]
    dma = pltpu.SemaphoreType.DMA
    return pl.pallas_call(
        functools.partial(feed_kernel, seq, fsdp),
        out_shape=(
            shape((rows, width), F32),
            shape((rows, width), BF16),
            shape((1, width), F32),
            shape(w_down.shape, BF16),
            shape((length, width), BF16),
            shape((width, inner), BF16),
            shape((width, inner), BF16),
        ),
        in_specs=[ANY] * 6 + [VMEM],
        out_specs=(VMEM,) * 4 + (ANY,) * 3,
        scratch_shapes=[
            pltpu.VMEM((length, width), BF16),
            pltpu.VMEM((inner, width), BF16),
            pltpu.VMEM((fsdp,) + w_down.shape, BF16),
            pltpu.VMEM((fsdp,) + w_down.shape if fsdp == 8 else (1, 16, 128), BF16),
            pltpu.VMEM((length, inner), F32),
            pltpu.VMEM((length, inner), F32),
            pltpu.VMEM((length, inner), BF16),
            pltpu.VMEM((length, inner), BF16),
            pltpu.VMEM((length, inner), BF16),
        ]
        + scatter_scratch(seq, rows, width)[:3]
        + [pltpu.VMEM((2, min(512, inner // 2), inner), BF16)]
        + load_scratch((w_gate, w_up, cot_all, middle))
        + [dma((1,)), dma((2,))]
        + [dma((n_copies(seq),))] * 4
        + line_scratch(fsdp) * 2
        + reduce_scratch(fsdp, *w_down.shape),
        compiler_params=params(1),
        name="feed",
    )(own_normed, cot_all, w_gate, w_up, middle, w_down, gains)


def backward_kernel(
    seq, fsdp, own_low, g_gate, g_up, w_out, attn, packed, lse, cosine, sine, w_qkv, hidden,
    d_middle, out_terms, middle, own_down, normed, ids_col, ids_row, gain, gain_two, d_input, output,
    own_qkv, own_gate, own_up, home_down, home_out, g_gain_one, g_gain_two, held_out, stage_out,
    got_out, held, stage, got, d_low, d_keys, d_vals, d_packed, grad_out, grad_qkv, mid_down,
    mid_out, own_out, parts, seq_parts, sums_own, fsdp_parts, *rest
):
    def take(count):
        nonlocal rest
        taken, rest = rest[:count], rest[count:]
        return taken

    rows, width = own_low.shape
    length = rows * seq
    groups = packed.shape[0] // 4
    ratio = fsdp // seq
    height, across = grad_out.shape[1:]
    tile, tall = tile_of(width, 512), tile_of(width, 512)
    me, row = lax.axis_index("seq"), lax.axis_index("fsdp")
    arrays = take(10)
    w_out, attn, packed, lse, cosine, sine, w_qkv, hidden, d_middle = loads(
        (w_out, attn, packed, lse, cosine, sine, w_qkv, hidden, d_middle),
        arrays[:9],
        arrays[9],
    )
    local = take(1)[0]
    terms = Load(out_terms, held_out, local.at[1])
    middle = Load(middle, output, local.at[2])
    meet(seq, fsdp)
    whole = Gather(seq, own_low, d_low, take(2))
    outs = Scatter(seq, held_out, stage_out, got_out, take(2))
    early = seq != 4
    if early:
        held = held_out
    sums = Scatter(seq, held, stage, got, take(2))
    part_sems = take(4)
    size = len(reduce_scratch(fsdp, 16, 128))
    line_gate = LineReduce(fsdp, g_gate, *take(size), mine=take(2))
    line_up = LineReduce(fsdp, g_up, *take(size), mine=take(2))
    line_out = LineReduce(fsdp, grad_out, *take(size))
    line_qkv = LineReduce(fsdp, grad_qkv, *take(size))
    moves = [
        Home(seq, fsdp, own_down, mid_down, home_down, take(3)),
        Home(seq, fsdp, own_out, mid_out, home_out, take(3)),
    ]
    whole.start()
    here = whole.local(local.at[0])
    here.start()
    line_gate.start()
    line_up.start()
    w_out, attn, packed, lse = w_out.get(), attn.get(), packed.get(), lse.get()
    cosine, sine = cosine.get(), sine.get()
    d_keys[...] = jnp.zeros_like(d_keys)
    d_vals[...] = jnp.zeros_like(d_vals)
    line_gate.pairs()
    here.wait()
    span = length // 2 + BLOCK

    def send_out():
        outs.send(lambda device, ref: terms.get())

    def out_grad():
        for k in range(seq):
            part = dot_tn(attn[...], d_low[:, k * across : (k + 1) * across]).astype(BF16)
            for down in range(ratio):
                grad_out[line_place(seq, fsdp, down, k)] = part[
                    down * height : (down + 1) * height
                ]
        line_out.start()

    def attend(index):
        steps = {k: functools.partial(whole.arrive, k) for k in range(1, seq)}
        at_step(index, steps)
        at_step(index, {seq - 1: out_grad})
        start = pl.multiple_of(whole.coming(index) * BLOCK, BLOCK)
        low = pl.multiple_of(jnp.maximum(start - length // 2, 0), BLOCK)
        part, keys = pl.ds(start, BLOCK), pl.ds(low, span)
        d_attn = dot_nt(d_low[part, :], w_out[...]).astype(BF16)
        bias = mask_bias(ids_col, ids_row, start, low, BLOCK, span)
        for group in range(groups):
            base = group * 2 * HEAD_DIM
            queries = jnp.concatenate(
                [packed[group * 4, part, :], packed[group * 4 + 1, part, :]], axis=0
            )
            d_wide = d_attn[:, base : base + 2 * HEAD_DIM]
            product = attn[part, base : base + 2 * HEAD_DIM].astype(F32) * d_wide.astype(F32)
            delta = jnp.concatenate(
                [
                    jnp.sum(product[:, :HEAD_DIM], axis=-1, keepdims=True),
                    jnp.sum(product[:, HEAD_DIM:], axis=-1, keepdims=True),
                ],
                axis=0,
            )
            d_out = jnp.concatenate([d_wide[:, :HEAD_DIM], d_wide[:, HEAD_DIM:]], axis=0)
            logs = jnp.concatenate(
                [
                    lse[part, group * 2 : group * 2 + 1],
                    lse[part, group * 2 + 1 : group * 2 + 2],
                ],
                axis=0,
            )
            key_rows = packed[group * 4 + 2, keys, :]
            scores = dot_nt(queries, key_rows) * SCALE_TWO + bias
            probs = jnp.exp2(scores - logs)
            d_probs = dot_nt(d_out, packed[group * 4 + 3, keys, :])
            d_scores = (probs * (d_probs - delta)).astype(BF16)
            d_vals[group, keys, :] += dot_tn(probs.astype(BF16), d_out)
            d_keys[group, keys, :] += dot_tn(d_scores, queries) * SCALE
            d_query = dot(d_scores, key_rows) * SCALE
            turned = [
                piece * cosine[part, :] - swap_halves(piece) * sine[part, :]
                for piece in (d_query[:BLOCK], d_query[BLOCK:])
            ]
            d_packed[part, group * 4 * HEAD_DIM : group * 4 * HEAD_DIM + 2 * HEAD_DIM] = (
                jnp.concatenate(turned, axis=1).astype(BF16)
            )
            if group == 0:
                at_step(index, {0: whole.forward})

    def passing(index):
        attend(index)
        at_step(
            index,
            {
                0: functools.partial(line_gate.forward, (0,)),
                1: second_step,
                2: third_step,
            },
        )

    def second_step():
        moves[0].start_plane()
        line_up.pairs()
        line_gate.forward((1,))

    def third_step():
        send_out()
        line_up.forward((0,))

    each(seq, 1, passing)
    whole.sent()
    normed = Load(normed, d_low, local.at[3])
    moves[0].finish_plane()
    moves[0].start_line()

    def last(at):
        part = pl.ds(at, BLOCK)
        for group in range(groups):
            d_key = d_keys[group, part, :]
            turned = d_key * cosine[part, :] - swap_halves(d_key) * sine[part, :]
            base = group * 4 * HEAD_DIM + 2 * HEAD_DIM
            d_packed[part, base : base + 2 * HEAD_DIM] = jnp.concatenate(
                [turned, d_vals[group, part, :]], axis=1
            ).astype(BF16)

    each(length, BLOCK, last)
    line_out.pairs()
    normed = normed.get()
    rows_each = grad_qkv.shape[1]

    per = 128 // math.gcd(128, rows_each)

    def weight(index):
        part = pl.ds(pl.multiple_of(index * per * rows_each, per * rows_each), per * rows_each)
        grad = dot_tn(normed[:, part], d_packed[...]).astype(BF16)
        for k in range(per):
            grad_qkv[index * per + k] = grad[k * rows_each : (k + 1) * rows_each]

    each(fsdp // per, 1, weight)
    line_qkv.start()
    w_qkv = w_qkv.get()

    def one(device, at):
        block = pl.ds(pl.multiple_of(device * rows, rows), rows)
        return dot_nt(d_packed[block, :], w_qkv[pl.ds(at, tile), :])

    def term(device, ref):
        def part(at):
            ref[:, pl.ds(at, tile)] = one(device, at).astype(BF16)

        each(width, tile, part)

    def finish_output():
        middle.get()
        outs.finish()

        def total_of(at):
            part = pl.ds(at, 128)
            output[part, :] = (
                output[part, :] + held_out[me, part, :].astype(F32) + outs.terms(part)
            )

        each(rows, 128, total_of)

    if early:
        finish_output()
    sums.send(
        term,
        [outs.forward, functools.partial(line_up.forward, (1,)), line_qkv.pairs],
    )

    def own(at):
        d_input[:, pl.ds(at, tile)] = one(me, at)

    each(width, tile, own)
    hidden, d_middle = hidden.get(), d_middle.get()
    line_out.forward()
    line_gate.finish(own_gate)
    sums.forward()
    line_qkv.forward((0,))
    line_up.finish(own_up)
    if not early:
        finish_output()
    line_out.finish(own_out)
    moves[1].start_plane()
    line_qkv.forward((1,))
    parts[0:1, :] = jnp.zeros((1, width), F32)
    parts[1:2, :] = gain_two[...]
    moves[1].finish_plane()
    moves[1].start_line()
    sums.finish()

    def norm(at):
        part = pl.ds(at, 128)
        values = hidden[part, :].astype(F32)
        grad = d_input[part, :] + sums.terms(part)
        scale = inv_rms(values)
        weighted = grad * gain[0:1, :]
        mean = jnp.mean(weighted * values, axis=-1, keepdims=True)
        parts[0:1, :] += jnp.sum(grad * values * scale, axis=0, keepdims=True)
        d_input[part, :] = d_middle[part, :] + scale * (
            weighted - values * (scale * scale) * mean
        )

    each(rows, 128, norm)
    first = [
        push(parts, seq_parts.at[k], part_sems[:2], k, peer)
        for k, peer in enumerate(others(seq))
    ]
    for copy in first:
        copy.start()
    moves[0].finish_line()
    for copy in first:
        copy.wait()
    total = parts[...]
    for k in range(seq - 1):
        total = total + seq_parts[k]
    sums_own[...] = total
    second = [
        push(
            sums_own,
            fsdp_parts.at[step - 1],
            part_sems[2:],
            step - 1,
            lax.rem(row + step, fsdp),
            "fsdp",
        )
        for step in range(1, fsdp)
    ]
    for copy in second:
        copy.start()
    moves[1].finish_line()
    line_qkv.finish(own_qkv)
    for copy in second:
        copy.wait()
    for step in range(1, fsdp):
        total = total + fsdp_parts[step - 1]
    share = g_gain_one.shape[1]
    turned = pltpu.roll(
        jnp.broadcast_to(total[:, None, :], (2, 8, width)).reshape(16, width),
        lax.rem(width - (row * seq + me) * share, width),
        1,
    )
    g_gain_one[...] = turned[0:1, :share]
    g_gain_two[...] = turned[8:9, :share]


def backward(
    seq, fsdp, own_low, g_gate, g_up, w_out, attn, packed, lse, cosine, sine, normed, w_qkv, hidden,
    d_middle, out_terms, middle, own_down, ids_col, ids_row, gain, gain_two
):
    rows, width = own_low.shape
    length = rows * seq
    inner = attn.shape[1]
    groups = packed.shape[0] // 4
    height, across = inner // (fsdp // seq), width // seq
    share = width // (seq * fsdp)
    shard = (width // fsdp, w_qkv.shape[1])
    count = home_count(seq, fsdp)
    dma = pltpu.SemaphoreType.DMA
    big = (w_out, attn, packed, lse, cosine, sine, w_qkv, hidden, d_middle)
    return pl.pallas_call(
        functools.partial(backward_kernel, seq, fsdp),
        out_shape=(
            shape((rows, width), F32),
            shape((rows, width), F32),
            shape(shard, BF16),
            shape(g_gate.shape[1:], BF16),
            shape(g_up.shape[1:], BF16),
            shape(own_down.shape, BF16),
            shape((height, across), BF16),
            shape((1, share), F32),
            shape((1, share), F32),
        ),
        in_specs=[ANY] * 16 + [VMEM] * 4,
        out_specs=(VMEM,) * 9,
        scratch_shapes=scatter_scratch(seq, rows, width)[:3]
        + [pltpu.VMEM((seq, rows, width) if seq == 4 else (1, 16, 128), BF16)]
        + scatter_scratch(seq, rows, width)[1:3]
        + [pltpu.VMEM((length, width), BF16)]
        + [pltpu.VMEM((groups, length, HEAD_DIM), F32)] * 2
        + [
            pltpu.VMEM((length, groups * 4 * HEAD_DIM), BF16),
            pltpu.VMEM((fsdp, height, across), BF16),
            pltpu.VMEM((fsdp,) + shard, BF16),
            pltpu.VMEM((count,) + own_down.shape, BF16),
            pltpu.VMEM((count, height, across), BF16),
            pltpu.VMEM((height, across), BF16),
            pltpu.VMEM((2, width), F32),
            pltpu.VMEM((seq - 1, 2, width), F32),
            pltpu.VMEM((2, width), F32),
            pltpu.VMEM((fsdp - 1, 2, width), F32),
        ]
        + load_scratch(big)
        + [dma((4,))]
        + [dma((n_copies(seq),))] * 6
        + [dma((seq - 1,))] * 2
        + [dma((fsdp - 1,))] * 2
        + (reduce_scratch(fsdp, *g_gate.shape[1:]) + mine_scratch(fsdp, *g_gate.shape[1:]))
        + (reduce_scratch(fsdp, *g_up.shape[1:]) + mine_scratch(fsdp, *g_up.shape[1:]))
        + reduce_scratch(fsdp, height, across)
        + reduce_scratch(fsdp, *shard)
        + home_sems(seq, fsdp) * 2,
        compiler_params=params(2),
        name="backward",
    )(
        own_low, g_gate, g_up, *big, out_terms, middle, own_down, normed, ids_col, ids_row, gain,
        gain_two,
    )


def widen_kernel(*refs):
    half = len(refs) // 2
    for src, dst in zip(refs[:half], refs[half:]):
        dst[...] = src[...].astype(F32)


def widen(*arrays):
    steps = 4 if all(array.shape[0] % 64 == 0 for array in arrays if array.shape[0] > 1) else 2
    specs = [
        pl.BlockSpec((array.shape[0] // steps, array.shape[1]), lambda i: (i, 0))
        if array.shape[0] > 1
        else pl.BlockSpec(array.shape, lambda i: (0, 0))
        for array in arrays
    ]
    return pl.pallas_call(
        widen_kernel,
        grid=(steps,),
        out_shape=tuple(shape(array.shape, F32) for array in arrays),
        in_specs=specs,
        out_specs=tuple(specs),
        compiler_params=params(),
        name="widen",
    )(*arrays)


def body(
    hidden_in, cotangent, segment_ids, w_qkv, w_out, w_gate, w_up, w_down, gain_attn, gain_mlp
):
    rows, width = hidden_in.shape
    fsdp = lax.axis_size("fsdp")
    seq = lax.axis_size("seq")
    length = rows * seq

    (
        ids_row, ids_col, gains, attn, lse, middle, normed_two, normed_one, cosine, sine, packed,
        rows_out, cols_qkv, cols_gate, cols_up, _, moved_down, cot_all,
    ) = forward(
        seq, fsdp, hidden_in, w_qkv, w_out, w_gate, w_up, w_down, cotangent, segment_ids,
        gain_attn.reshape(1, -1), gain_mlp.reshape(1, -1),
    )
    d_middle, own_low, part_two, own_down, out_terms, g_gate, g_up = feed(
        seq, fsdp, normed_two, cot_all, cols_gate.reshape(width, -1), cols_up.reshape(width, -1),
        middle, moved_down, gains,
    )
    out_terms = out_terms.reshape(seq, rows, width)
    g_up = g_up.reshape((fsdp,) + w_up.shape)
    results = backward(
        seq, fsdp, own_low, g_gate.reshape((fsdp,) + w_gate.shape), g_up, rows_out, attn, packed,
        lse, cosine, sine, normed_one, cols_qkv.reshape(width, -1), hidden_in, d_middle, out_terms,
        middle, own_down, ids_col, ids_row, gains, part_two,
    )
    d_input, output, g_qkv, g_gate, g_up, g_down, g_out, g_gain_one, g_gain_two = widen(*results)
    return (
        output, d_input, g_qkv, g_out, g_gate, g_up, g_down, g_gain_one.reshape(-1),
        g_gain_two.reshape(-1),
    )


def solution(mesh):
    both = P(("fsdp", "seq"), None)
    split = P("fsdp", "seq")
    gain = P(("fsdp", "seq"))
    in_specs = (both, both, split, split, split, split, split, split, gain, gain)
    out_specs = (both, both, split, split, split, split, split, gain, gain)
    return jax.shard_map(body, mesh=mesh, in_specs=in_specs, out_specs=out_specs, check_vma=False)
```

profile of v0, /device:TPU:0, one launch (start us, length us, event | category | flops | bytes accessed | tf_op | source)
XLA Modules:
  0.0 308.7 jit_solution(7973986367086167654)
XLA Ops:
  0.6 108.1 %forward.1 = (s32[1,1024]{1,0:T(1,128)}, s32[1024,1]{1,0:T(8,128)}, f32[2,1536]{1,0:T(2,128)}, bf16[1024,384]{1,0:T(8,128)(2,1)}, f32[1024,128]{1,0:T(8,128)}, /...) custom-call(bf16[256,1536]{1,0:T(8,128)(2,1)} %hidden.3, ...), custom_call_target="tpu_custom_call" | custom-call | tf_op jit(solution)/shard_map/forward/pallas_call | solution.py:1077
  108.7 86.4 %feed.1 = (f32[256,1536]{1,0:T(8,128)}, bf16[256,1536]{1,0:T(8,128)(2,1)}, f32[1,1536]{1,0:T(1,128)}, bf16[512,384]{1,0:T(8,128)(2,1)}, bf16[1024,1536]{1,0:T(8,...) custom-call(bf16[256,1536]{1,0:T(8,128)(2,1)} %get-tuple-element.51.own_normed, ...), custom_call_target="tpu_custom_call" | custom-call | tf_op jit(solution)/shard_map/feed/pallas_call | solution.py:1313
  195.1 107.9 %backward.1 = (f32[256,1536]{1,0:T(8,128)}, f32[256,1536]{1,0:T(8,128)}, bf16[192,768]{1,0:T(8,128)(2,1)}, bf16[192,1024]{1,0:T(8,128)(2,1)}, bf16[192,1024]{1,0...) custom-call(bf16[256,1536]{1,0:T(8,128)(2,1)} %get-tuple-element.58.own, ...), custom_call_target="tpu_custom_call" | custom-call | tf_op jit(solution)/shard_map/backward/pallas_call | solution.py:1640
  303.0 5.5 %widen.1 = (f32[256,1536]{1,0:T(8,128)}, f32[256,1536]{1,0:T(8,128)}, f32[192,768]{1,0:T(8,128)}, f32[192,1024]{1,0:T(8,128)}, f32[192,1024]{1,0:T(8,128)}, /*in...) custom-call(f32[256,1536]{1,0:T(8,128)} %get-tuple-element.75.refs_0_, ...), custom_call_target="tpu_custom_call" | custom-call | tf_op jit(solution)/shard_map/widen/pallas_call | solution.py:1704
where the time goes:
time: 310 us; the launch traced here: 309 us
  Pallas kernels  308 us (99%)
    pallas_call x1, Pallas kernels, forward(): pl.pallas_call(functools.partial(forward_kernel, seq, fsdp), out_shape=(s...  108 us
    pallas_call x1, Pallas kernels, backward(): pl.pallas_call(functools.partial(backward_kernel, seq, fsdp), out_shape=(...  108 us
    pallas_call x1, Pallas kernels, feed(): pl.pallas_call(functools.partial(feed_kernel, seq, fsdp), out_shape=(shap...  86.4 us

commit v1 on v0

--- a/solution.py
+++ b/solution.py
@@ -1132,7 +1132,7 @@
 
 def feed_kernel(
     seq, fsdp, own_normed, cot_all, w_gate, w_up, middle, w_down, gains, d_middle, own_low, d_gain,
-    own_down, out_terms, g_gate, g_up, normed, whole_down, blocks, g_down, gate, up, hid, d_gate,
+    own_down, out_terms, down_out, g_gate, g_up, normed, whole_down, blocks, g_down, gate, up, hid, d_gate,
     d_up, held, stage, got, grad_tiles, *rest
 ):
     arrays, rest = rest[:5], rest[5:]
@@ -1270,6 +1270,9 @@
         if left is d_gate:
             line.forward((1,))
 
+    terms_out = pltpu.make_async_copy(hid if seq == 4 else normed, out_terms, local.at[0])
+    down_copy = pltpu.make_async_copy(whole_down, down_out, local.at[1])
+
     def outward(index):
         block = pl.ds(pl.multiple_of(index * rows, rows), rows)
 
@@ -1279,8 +1282,10 @@
 
         each(width, tile, part)
 
-    each(seq, 1, outward)
-    terms_out = pltpu.make_async_copy(normed, out_terms, local.at[0])
+    if seq == 4:
+        down_copy.start()
+    else:
+        each(seq, 1, outward)
     terms_out.start()
     sums.finish()
     d_gain[...] = jnp.zeros_like(d_gain)
@@ -1303,6 +1308,8 @@
     each(rows, 128, norm)
     line.finish(own_down)
     terms_out.wait()
+    if seq == 4:
+        down_copy.wait()
 
 
 def feed(seq, fsdp, own_normed, cot_all, w_gate, w_up, middle, w_down, gains):
@@ -1317,12 +1324,13 @@
             shape((rows, width), BF16),
             shape((1, width), F32),
             shape(w_down.shape, BF16),
-            shape((length, width), BF16),
+            shape((length, inner if seq == 4 else width), BF16),
+            shape((inner, width) if seq == 4 else (16, 128), BF16),
             shape((width, inner), BF16),
             shape((width, inner), BF16),
         ),
         in_specs=[ANY] * 6 + [VMEM],
-        out_specs=(VMEM,) * 4 + (ANY,) * 3,
+        out_specs=(VMEM,) * 4 + (ANY,) * 4,
         scratch_shapes=[
             pltpu.VMEM((length, width), BF16),
             pltpu.VMEM((inner, width), BF16),
@@ -1337,7 +1345,7 @@
         + scatter_scratch(seq, rows, width)[:3]
         + [pltpu.VMEM((2, min(512, inner // 2), inner), BF16)]
         + load_scratch((w_gate, w_up, cot_all, middle))
-        + [dma((1,)), dma((2,))]
+        + [dma((2,)), dma((2,))]
         + [dma((n_copies(seq),))] * 4
         + line_scratch(fsdp) * 2
         + reduce_scratch(fsdp, *w_down.shape),
@@ -1348,10 +1356,10 @@
 
 def backward_kernel(
     seq, fsdp, own_low, g_gate, g_up, w_out, attn, packed, lse, cosine, sine, w_qkv, hidden,
-    d_middle, out_terms, middle, own_down, normed, ids_col, ids_row, gain, gain_two, d_input, output,
+    d_middle, out_terms, w_down, middle, own_down, normed, ids_col, ids_row, gain, gain_two, d_input, output,
     own_qkv, own_gate, own_up, home_down, home_out, g_gain_one, g_gain_two, held_out, stage_out,
     got_out, held, stage, got, d_low, d_keys, d_vals, d_packed, grad_out, grad_qkv, mid_down,
-    mid_out, own_out, parts, seq_parts, sums_own, fsdp_parts, *rest
+    mid_out, own_out, parts, seq_parts, sums_own, fsdp_parts, hid, *rest
 ):
     def take(count):
         nonlocal rest
@@ -1372,7 +1380,11 @@
         arrays[9],
     )
     local = take(1)[0]
-    terms = Load(out_terms, held_out, local.at[1])
+    if seq == 4:
+        terms = Load(out_terms, hid, local.at[1])
+        w_down = Load(w_down, held, local.at[4])
+    else:
+        terms = Load(out_terms, held_out, local.at[1])
     middle = Load(middle, output, local.at[2])
     meet(seq, fsdp)
     whole = Gather(seq, own_low, d_low, take(2))
@@ -1402,10 +1414,27 @@
     d_vals[...] = jnp.zeros_like(d_vals)
     line_gate.pairs()
     here.wait()
+    if seq == 4:
+        w_down.get()
+        terms.get()
+
+        def outward(index):
+            block = pl.ds(pl.multiple_of(index * rows, rows), rows)
+
+            def part(at):
+                cols = pl.ds(at, tile)
+                weight = held[:, :, cols].reshape(hid.shape[1], tile)
+                held_out[index, :, cols] = dot(hid[block, :], weight).astype(BF16)
+
+            each(width, tile, part)
+
+        each(seq, 1, outward)
     span = length // 2 + BLOCK
 
     def send_out():
-        outs.send(lambda device, ref: terms.get())
+        if seq != 4:
+            terms.get()
+        outs.send(lambda device, ref: None)
 
     def out_grad():
         for k in range(seq):
@@ -1625,7 +1654,7 @@
 
 def backward(
     seq, fsdp, own_low, g_gate, g_up, w_out, attn, packed, lse, cosine, sine, normed, w_qkv, hidden,
-    d_middle, out_terms, middle, own_down, ids_col, ids_row, gain, gain_two
+    d_middle, out_terms, w_down, middle, own_down, ids_col, ids_row, gain, gain_two
 ):
     rows, width = own_low.shape
     length = rows * seq
@@ -1650,7 +1679,7 @@
             shape((1, share), F32),
             shape((1, share), F32),
         ),
-        in_specs=[ANY] * 16 + [VMEM] * 4,
+        in_specs=[ANY] * 17 + [VMEM] * 4,
         out_specs=(VMEM,) * 9,
         scratch_shapes=scatter_scratch(seq, rows, width)[:3]
         + [pltpu.VMEM((seq, rows, width) if seq == 4 else (1, 16, 128), BF16)]
@@ -1668,9 +1697,10 @@
             pltpu.VMEM((seq - 1, 2, width), F32),
             pltpu.VMEM((2, width), F32),
             pltpu.VMEM((fsdp - 1, 2, width), F32),
+            pltpu.VMEM(out_terms.shape if seq == 4 else (16, 128), BF16),
         ]
         + load_scratch(big)
-        + [dma((4,))]
+        + [dma((5,))]
         + [dma((n_copies(seq),))] * 6
         + [dma((seq - 1,))] * 2
         + [dma((fsdp - 1,))] * 2
@@ -1682,7 +1712,7 @@
         compiler_params=params(2),
         name="backward",
     )(
-        own_low, g_gate, g_up, *big, out_terms, middle, own_down, normed, ids_col, ids_row, gain,
+        own_low, g_gate, g_up, *big, out_terms, w_down, middle, own_down, normed, ids_col, ids_row, gain,
         gain_two,
     )
 
@@ -1694,7 +1724,7 @@
 
 
 def widen(*arrays):
-    steps = 4 if all(array.shape[0] % 64 == 0 for array in arrays if array.shape[0] > 1) else 2
+    steps = 2
     specs = [
         pl.BlockSpec((array.shape[0] // steps, array.shape[1]), lambda i: (i, 0))
         if array.shape[0] > 1
@@ -1727,15 +1757,18 @@
         seq, fsdp, hidden_in, w_qkv, w_out, w_gate, w_up, w_down, cotangent, segment_ids,
         gain_attn.reshape(1, -1), gain_mlp.reshape(1, -1),
     )
-    d_middle, own_low, part_two, own_down, out_terms, g_gate, g_up = feed(
+    d_middle, own_low, part_two, own_down, out_terms, rows_down, g_gate, g_up = feed(
         seq, fsdp, normed_two, cot_all, cols_gate.reshape(width, -1), cols_up.reshape(width, -1),
         middle, moved_down, gains,
     )
-    out_terms = out_terms.reshape(seq, rows, width)
+    if seq == 4:
+        rows_down = rows_down.reshape(seq, rows, width)
+    else:
+        out_terms = out_terms.reshape(seq, rows, width)
     g_up = g_up.reshape((fsdp,) + w_up.shape)
     results = backward(
         seq, fsdp, own_low, g_gate.reshape((fsdp,) + w_gate.shape), g_up, rows_out, attn, packed,
-        lse, cosine, sine, normed_one, cols_qkv.reshape(width, -1), hidden_in, d_middle, out_terms,
+        lse, cosine, sine, normed_one, cols_qkv.reshape(width, -1), hidden_in, d_middle, out_terms, rows_down,
         middle, own_down, ids_col, ids_row, gains, part_two,
     )
     d_input, output, g_qkv, g_gate, g_up, g_down, g_out, g_gain_one, g_gain_two = widen(*results)

time: 310 us -> 309 us (level)
  no operation moved by 1% of the time
where the time goes in v1:
time: 309 us; the launch traced here: 308 us
  Pallas kernels  307 us (99%)
    pallas_call x1, Pallas kernels, forward(): pl.pallas_call(functools.partial(forward_kernel, seq, fsdp), out_shape=(s...  108 us
    pallas_call x1, Pallas kernels, backward(): pl.pallas_call(functools.partial(backward_kernel, seq, fsdp), out_shape=(...  108 us
    pallas_call x1, Pallas kernels, feed(): pl.pallas_call(functools.partial(feed_kernel, seq, fsdp), out_shape=(shap...  86.3 us

profile of v1, /device:TPU:0, one launch (start us, length us, event | category | flops | bytes accessed | tf_op | source)
XLA Modules:
  0.0 307.9 jit_solution(1343351458476457991)
XLA Ops:
  0.6 108.1 %forward.1 = (s32[1,1024]{1,0:T(1,128)}, s32[1024,1]{1,0:T(8,128)}, f32[2,1536]{1,0:T(2,128)}, bf16[1024,384]{1,0:T(8,128)(2,1)}, f32[1024,128]{1,0:T(8,128)}, /...) custom-call(bf16[256,1536]{1,0:T(8,128)(2,1)} %hidden.3, ...), custom_call_target="tpu_custom_call" | custom-call | tf_op jit(solution)/shard_map/forward/pallas_call | solution.py:1077
  108.7 86.3 %feed.1 = (f32[256,1536]{1,0:T(8,128)}, bf16[256,1536]{1,0:T(8,128)(2,1)}, f32[1,1536]{1,0:T(1,128)}, bf16[512,384]{1,0:T(8,128)(2,1)}, bf16[1024,1024]{1,0:T(8,...) custom-call(bf16[256,1536]{1,0:T(8,128)(2,1)} %get-tuple-element.52.own_normed, ...), custom_call_target="tpu_custom_call" | custom-call | tf_op jit(solution)/shard_map/feed/pallas_call | solution.py:1320
  195.1 108.0 %backward.1 = (f32[256,1536]{1,0:T(8,128)}, f32[256,1536]{1,0:T(8,128)}, bf16[192,768]{1,0:T(8,128)(2,1)}, bf16[192,1024]{1,0:T(8,128)(2,1)}, bf16[192,1024]{1,0...) custom-call(bf16[256,1536]{1,0:T(8,128)(2,1)} %get-tuple-element.59.own, ...), custom_call_target="tpu_custom_call" | custom-call | tf_op jit(solution)/shard_map/backward/pallas_call | solution.py:1669
  303.1 4.6 %widen.1 = (f32[256,1536]{1,0:T(8,128)}, f32[256,1536]{1,0:T(8,128)}, f32[192,768]{1,0:T(8,128)}, f32[192,1024]{1,0:T(8,128)}, f32[192,1024]{1,0:T(8,128)}, /*in...) custom-call(f32[256,1536]{1,0:T(8,128)} %get-tuple-element.77.refs_0_, ...), custom_call_target="tpu_custom_call" | custom-call | tf_op jit(solution)/shard_map/widen/pallas_call | solution.py:1734
